TPU v7x, 128 devices: a whole 4x4x4 slice. The times are simulated.
128 devices in a mesh: gx: 8 (over x, core), yz: 16 (over z, y).
Axes of the slice: x: 4, y: 4, z: 4, core: 2. Of those that a mesh axis runs over, the one named last changes fastest.
Arguments:
- displacement: float32 [3, 64, 256, 2048], P(None, 'gx', 'yz'), may hold values from -1.2 to 1.2
- force: float32 [3, 64, 256, 2048], P(None, 'gx', 'yz'), may hold values from -1.2 to 1.2
- damage: float32 [64, 256, 2048], P('gx', 'yz'), may hold values from 0 to 0.6
- history_old: float32 [64, 256, 2048], P('gx', 'yz'), may hold values from 0 to 0.5
- material: int32 [64, 256, 2048], P('gx', 'yz'), may hold values from 0 to 3
- patch_ids: int32 [128, 12], P(('gx', 'yz')), may hold values from 0 to 15, as said below
- owners: int32 [128, 12, 1], P(('gx', 'yz')), may hold values from 0 to 15; in each aligned block of 12 rows (0 to 11, 12 to 23, ..., all dimensions but the last counted through in order) at most 2 rows name the same one
- toughness: float32 [128, 16, 2, 8, 16, 128], P(('gx', 'yz')), may hold values from 0.5 to 2
Outputs:
- new_displacement: float32 [3, 64, 256, 2048], P(None, 'gx', 'yz')
- history: float32 [64, 256, 2048], P('gx', 'yz')
- new_damage: float32 [64, 256, 2048], P('gx', 'yz')
Inputs may be any that keep to these rules, and one draw needn't show every extreme that they name: `owners`: the entries of one device name one owner at most 2 times, and exactly 2 times in some devices. `patch_ids`: the 12 entries of one device are distinct.
All inputs are finite; a program needn't handle non-finite values.
Results may differ from a plain program's by a relative error of at most 0.0001.
Values sent between devices are 32-bit elements; how exact they have to be, the bound alone decides.
A program may use at most 128 MiB of HBM per device.

v0:
```python
import jax
import jax.numpy as jnp
from jax import lax
from jax.experimental import pallas as pl
from jax.experimental.pallas import tpu as pltpu
from jax.sharding import PartitionSpec as P

PZ = 128
PL = 12
CAP = 2
SWEEPS = 8
SPRING = 0.05
RELAX = 0.8
LENGTH = 2.0

CX = 8
CY = 16
NZ = 16
N_GX = 8
N_YZ = 16
SIDE = 4
R0 = 8
MESH = pl.DeviceIdType.MESH
F32 = jnp.float32

MOVES = [(1, 0), (3, 0), (2, 0), (0, 1), (0, 3), (1, 1), (3, 3), (1, 3), (3, 1),
         (2, 1), (2, 3), (0, 2), (1, 2), (3, 2), (2, 2)]
GROUPS = (6, 10, 15)
LATE = 4
FIRST = len(MOVES) - LATE
BATCH = 4
STAGES = ((4, 0), (4, 2), (2, 3), (2, 4))


def modulus(material):
    return jnp.where(
        material == 0,
        F32(1.0),
        jnp.where(material == 1, F32(0.5), jnp.where(material == 2, F32(4.0), F32(0.25))),
    )


def lane_masks():
    lane = lax.broadcasted_iota(jnp.int32, (8, PZ), 1)
    return lane == 0, lane == PZ - 1


def mechanics(ids, own, disp, force, damage, hist_old, material, tough, u2, hist, dmg, res, order,
              u0, u1, stiff, fbuf, mat, coef, wback, wahead, recv, home, late, grid_mat, line_mat, dcur, acur, bcur, keys,
              ld_sem, s_send, s_recv, u_send, u_recv, t_send, t_recv):
    gx = lax.axis_index("gx")
    yz = lax.axis_index("yz")
    my_z = yz // SIDE
    my_y = yz % SIDE
    x_low = gx > 0
    x_high = gx < N_GX - 1
    y_low = yz > 0
    y_high = yz < N_YZ - 1
    peers = [
        ((gx + N_GX - 1) % N_GX, yz),
        ((gx + 1) % N_GX, yz),
        (gx, (yz + N_YZ - 1) % N_YZ),
        (gx, (yz + 1) % N_YZ),
    ]
    exists = [x_low, x_high, y_low, y_high]

    def load(src, dst, sem):
        return pltpu.make_async_copy(src, dst, sem)

    zeros = jnp.zeros((8, PZ), F32)

    def clear_x(plane):
        def one(k, _):
            for half in range(2):
                rows = pl.ds(R0 + 8 * half, 8)
                stiff[plane, k, rows, :] = zeros
                for c in range(3):
                    u0[c, plane, k, rows, :] = zeros
                    u1[c, plane, k, rows, :] = zeros
                    u2[c, plane, k, rows, :] = zeros
            return 0
        lax.fori_loop(1, NZ + 1, one, 0)

    def clear_y(row):
        def one(x, _):
            for k in range(1, NZ + 1):
                rows = pl.ds(row, 8)
                stiff[x, k, rows, :] = zeros
                for c in range(3):
                    u0[c, x, k, rows, :] = zeros
                    u1[c, x, k, rows, :] = zeros
                    u2[c, x, k, rows, :] = zeros
            return 0
        lax.fori_loop(1, CX + 1, one, 0)

    def clear_z(x, _):
        for k in (0, NZ + 1):
            for half in range(2):
                rows = pl.ds(R0 + 8 * half, 8)
                stiff[x, k, rows, :] = zeros
                for c in range(3):
                    u0[c, x, k, rows, :] = zeros
                    u1[c, x, k, rows, :] = zeros
                    u2[c, x, k, rows, :] = zeros
        return 0

    lax.fori_loop(1, CX + 1, clear_z, 0)
    pl.when(jnp.logical_not(x_low))(lambda: clear_x(0))
    pl.when(jnp.logical_not(x_high))(lambda: clear_x(CX + 1))
    pl.when(jnp.logical_not(y_low))(lambda: clear_y(0))
    pl.when(jnp.logical_not(y_high))(lambda: clear_y(R0 + CY))

    def zs(k):
        return pl.ds(pl.multiple_of(k * PZ, PZ), PZ)

    def start_first(k, _):
        load(damage.at[:, :, zs(k)], dmg.at[:, k], ld_sem.at[0]).start()
        load(material.at[:, :, zs(k)], mat.at[:, k], ld_sem.at[1]).start()
        return 0

    def start_second(k, _):
        load(disp.at[:, :, :, zs(k)], u0.at[:, pl.ds(1, CX), k + 1, pl.ds(R0, CY), :], ld_sem.at[2]).start()
        load(force.at[:, :, :, zs(k)], fbuf.at[:, :, k], ld_sem.at[3]).start()
        load(hist_old.at[:, :, zs(k)], hist.at[:, k], ld_sem.at[4]).start()
        return 0

    lax.fori_loop(0, NZ, start_first, 0)
    lax.fori_loop(0, NZ, start_second, 0)
    mine = load(tough.at[yz], home, ld_sem.at[5])
    mine.start()

    barrier = pltpu.get_barrier_semaphore()
    for d in range(1, N_YZ):
        pl.semaphore_signal(barrier, inc=1, device_id=(gx, (yz + d) % N_YZ), device_id_type=MESH)
    for peer in peers[:2]:
        pl.semaphore_signal(barrier, inc=1, device_id=peer, device_id_type=MESH)
    pl.semaphore_wait(barrier, N_YZ + 1)

    def remote(src, dst, send, recv_s, peer):
        return pltpu.make_async_remote_copy(
            src_ref=src, dst_ref=dst, send_sem=send, recv_sem=recv_s,
            device_id=peer, device_id_type=MESH)

    for d in range(4):
        @pl.when(exists[d])
        def _(d=d):
            def one(k, _):
                if d == 0:
                    src, dst = disp.at[:, 0, :, zs(k)], u0.at[:, CX + 1, k + 1, pl.ds(R0, CY), :]
                elif d == 1:
                    src, dst = disp.at[:, CX - 1, :, zs(k)], u0.at[:, 0, k + 1, pl.ds(R0, CY), :]
                elif d == 2:
                    src = disp.at[:, :, pl.ds(0, 1), zs(k)]
                    dst = u0.at[:, pl.ds(1, CX), k + 1, pl.ds(R0 + CY, 1), :]
                else:
                    src = disp.at[:, :, pl.ds(CY - 1, 1), zs(k)]
                    dst = u0.at[:, pl.ds(1, CX), k + 1, pl.ds(R0 - 1, 1), :]
                remote(src, dst, u_send.at[0, d], u_recv.at[0, d], peers[d]).start()
                return 0
            lax.fori_loop(0, NZ, one, 0)

    ZIN = pl.ds(1, NZ)

    def s_copy(d, x):
        if d == 0:
            src, dst = stiff.at[1, ZIN, pl.ds(R0, CY), :], stiff.at[CX + 1, ZIN, pl.ds(R0, CY), :]
        elif d == 1:
            src, dst = stiff.at[CX, ZIN, pl.ds(R0, CY), :], stiff.at[0, ZIN, pl.ds(R0, CY), :]
        elif d == 2:
            src, dst = stiff.at[x, ZIN, pl.ds(R0, 1), :], stiff.at[x, ZIN, pl.ds(R0 + CY, 1), :]
        else:
            src, dst = stiff.at[x, ZIN, pl.ds(R0 + CY - 1, 1), :], stiff.at[x, ZIN, pl.ds(R0 - 1, 1), :]
        return remote(src, dst, s_send.at[d], s_recv.at[d], peers[d])

    def u_copy(buf, r, d, x):
        if d == 0:
            src, dst = buf.at[:, 1, ZIN, pl.ds(R0, CY), :], buf.at[:, CX + 1, ZIN, pl.ds(R0, CY), :]
        elif d == 1:
            src, dst = buf.at[:, CX, ZIN, pl.ds(R0, CY), :], buf.at[:, 0, ZIN, pl.ds(R0, CY), :]
        elif d == 2:
            src, dst = buf.at[:, x, ZIN, pl.ds(R0, 1), :], buf.at[:, x, ZIN, pl.ds(R0 + CY, 1), :]
        else:
            src, dst = buf.at[:, x, ZIN, pl.ds(R0 + CY - 1, 1), :], buf.at[:, x, ZIN, pl.ds(R0 - 1, 1), :]
        return remote(src, dst, u_send.at[r, d], u_recv.at[r, d], peers[d])

    every = pl.ds(1, CX)

    def send_planes(i, x, copy, dirs):
        for d in dirs:
            if d == 0:
                cond = jnp.logical_and(exists[d], i == 0)
            elif d == 1:
                cond = jnp.logical_and(exists[d], i == 1)
            else:
                cond = exists[d]
            pl.when(cond)(lambda d=d: copy(d, x).start())

    def wait_recvs(copy, dirs):
        for d in dirs:
            pl.when(exists[d ^ 1])(lambda d=d: copy(d, every).wait_recv())

    def wait_sends(copy, dirs):
        for d in dirs:
            pl.when(exists[d])(lambda d=d: copy(d, every).wait_send())

    def t_copy(m):
        dz, dy = MOVES[m]
        dst = (my_z + dz) % SIDE * SIDE + (my_y + dy) % SIDE
        slots = recv.at[yz] if m < FIRST else late[m - FIRST]
        return remote(tough.at[dst], slots, t_send.at[m], t_recv.at[m], (gx, dst))

    def plane_of(i):
        return 1 + (7 * i) % CX

    low_edge, high_edge = lane_masks()
    stencils(grid_mat, line_mat)

    def bytes_wait(src, dst, sem):
        load(src, dst, sem).wait()

    bytes_wait(dmg, dmg, ld_sem.at[0])
    bytes_wait(mat, mat, ld_sem.at[1])

    def stiff_plane(i, _):
        x = plane_of(i)
        for half in range(2):
            for k in range(NZ):
                part = (x - 1, k, pl.ds(8 * half, 8), slice(None))
                mod = modulus(mat[part])
                gap = 1.0 - dmg[part]
                stiff[x, k + 1, pl.ds(R0 + 8 * half, 8), :] = (0.5 * mod) * (gap * gap + 0.001)
        send_planes(i, x, s_copy, (0, 1, 2, 3))
        return 0

    lax.fori_loop(0, CX, stiff_plane, 0)

    def shifted(load_tile, k, mid):
        before = pltpu.roll(jnp.where(high_edge, load_tile(k - 1), mid), 1, 1)
        after = pltpu.roll(jnp.where(low_edge, load_tile(k + 1), mid), PZ - 1, 1)
        return before, after

    def z_faces(x, _):
        for half in range(2):
            here = pl.ds(R0 + 8 * half, 8)
            for k in range(1, NZ + 1):
                s = stiff[x, k, here, :]
                before, after = shifted(lambda kk: stiff[x, kk, here, :], k, s)
                part = (x - 1, k - 1, pl.ds(8 * half, 8), slice(None))
                wback[part] = s + before
                wahead[part] = s + after
        return 0


    for m in range(0, GROUPS[0]):
        t_copy(m).start()
    lax.fori_loop(1, CX + 1, z_faces, 0)

    bytes_wait(fbuf, fbuf, ld_sem.at[2])
    bytes_wait(fbuf, fbuf, ld_sem.at[3])
    bytes_wait(hist, hist, ld_sem.at[4])

    def u0_wait(d):
        return u_copy(u0, 0, d, every)

    wait_recvs(s_copy, (0, 1, 2, 3))
    wait_recvs(lambda d, x: u_copy(u0, 0, d, x), (0, 1, 2, 3))

    def relax(old, new, first, r, dirs):
        def plane(i, _):
            x = plane_of(i)
            for half in range(2):
                row = R0 + 8 * half
                here, back, ahead = pl.ds(row, 8), pl.ds(row - 1, 8), pl.ds(row + 1, 8)
                for k in range(1, NZ + 1):
                    part = (x - 1, k - 1, pl.ds(8 * half, 8), slice(None))
                    s = stiff[x, k, here, :]
                    w = [
                        s + stiff[x - 1, k, here, :],
                        s + stiff[x + 1, k, here, :],
                        s + stiff[x, k, back, :],
                        s + stiff[x, k, ahead, :],
                        wback[part],
                        wahead[part],
                    ]
                    if first:
                        total = (w[0] + w[1]) + (w[2] + w[3]) + (w[4] + w[5])
                        scale = RELAX / ((2.0 * SPRING) * s + total)
                        coef[part] = scale
                    else:
                        scale = coef[part]
                    for c in range(3):
                        u = old[c, x, k, here, :]
                        before, after = shifted(lambda kk: old[c, x, kk, here, :], k, u)
                        acc = w[0] * old[c, x - 1, k, here, :] + w[1] * old[c, x + 1, k, here, :]
                        acc = acc + (w[2] * old[c, x, k, back, :] + w[3] * old[c, x, k, ahead, :])
                        acc = acc + (w[4] * before + w[5] * after)
                        drive = fbuf[(c,) + part] + acc
                        new[c, x, k, here, :] = (1.0 - RELAX) * u + scale * drive
            send_planes(i, x, lambda d, xx: u_copy(new, r, d, xx), dirs)
            return 0
        lax.fori_loop(0, CX, plane, 0)

    relax(u0, u1, True, 1, (0, 1, 2, 3))
    for m in range(GROUPS[0], GROUPS[1]):
        t_copy(m).start()
    wait_recvs(lambda d, x: u_copy(u1, 1, d, x), (0, 1, 2, 3))

    relax(u1, u2, False, 2, (0, 2))
    for m in range(GROUPS[1], GROUPS[2]):
        t_copy(m).start()

    wait_recvs(lambda d, x: u_copy(u2, 2, d, x), (0, 2))

    def energy_plane(i, _):
        x = i + 1
        for half in range(2):
            row = R0 + 8 * half
            here, ahead = pl.ds(row, 8), pl.ds(row + 1, 8)
            for k in range(1, NZ + 1):
                part = (i, k - 1, pl.ds(8 * half, 8), slice(None))
                total = None
                for c in range(3):
                    u = u2[c, x, k, here, :]
                    after = jnp.where(low_edge, u2[c, x, k + 1, here, :], u)
                    a = u2[c, x + 1, k, here, :] - u
                    b = u2[c, x, k, ahead, :] - u
                    g = pltpu.roll(after, PZ - 1, 1) - u
                    term = a * a + b * b + g * g
                    total = term if total is None else total + term
                energy = (0.5 * modulus(mat[part])) * total
                hist[part] = jnp.maximum(hist[part], energy)
        return 0

    lax.fori_loop(0, CX, energy_plane, 0)

    def fill_key(j, _):
        owner = own[0, j]
        back_z = (my_z - owner // SIDE + SIDE) % SIDE
        back_y = (my_y - owner % SIDE + SIDE) % SIDE
        key = 0
        for c in range(LATE):
            dz, dy = MOVES[FIRST + c]
            key = key + jnp.where(jnp.logical_and(back_z == dz, back_y == dy), c + 1, 0)
        keys[0, j] = key
        slot = lax.fori_loop(0, j, lambda i, n: n + jnp.where(own[0, i] == owner, 1, 0), 0)
        keys[1, j] = jnp.minimum(slot, CAP - 1)
        return 0

    lax.fori_loop(0, PL, fill_key, 0)

    def fill_place(j, _):
        key = keys[0, j]

        def count(i, n):
            other = keys[0, i]
            before = jnp.logical_or(other < key, jnp.logical_and(other == key, i < j))
            return n + jnp.where(before, 1, 0)
        keys[2, j] = lax.fori_loop(0, PL, count, 0)
        return 0

    lax.fori_loop(0, PL, fill_place, 0)

    def fill_order(q, _):
        keys[3, q] = lax.fori_loop(0, PL, lambda i, n: n + jnp.where(keys[2, i] == q, i, 0), 0)
        return 0

    lax.fori_loop(0, PL, fill_order, 0)

    def fill_ids(q, _):
        order[0, q] = ids[0, keys[3, q]]
        return 0

    lax.fori_loop(0, PL, fill_ids, 0)

    mine.wait()
    cells = CX * CY

    def batch(first, size, arrived):
        def setup(b, _):
            q = first + b
            j = keys[3, q]
            key, slot, p = keys[0, j], keys[1, j], ids[0, j]
            g = jnp.where(own[0, j] == yz, home[slot], recv[own[0, j], slot])
            for c in range(arrived):
                g = jnp.where(key == c + 1, late[c][slot], g)
            g = g.reshape(cells, PZ)
            h2 = (2.0 * hist[:, p]).reshape(cells, PZ)
            g2 = g * LENGTH
            inv = 1.0 / (g / LENGTH + h2 + 6.0 * g2)
            acur[b] = h2 * inv
            bcur[b] = g2 * inv
            dcur[b] = dmg[:, p].reshape(cells, PZ)
            return 0

        lax.fori_loop(0, size, setup, 0)
        for b in range(size):
            res[first + b] = dcur[b].reshape(CX, CY, PZ)

        def sweep(step, _):
            line = line_mat[...]
            d = dcur[pl.ds(0, size)].reshape(size * cells, PZ)
            hi = d.astype(jnp.bfloat16)
            lo = (d - hi.astype(F32)).astype(jnp.bfloat16)
            zs_ = jnp.dot(jnp.concatenate([hi, lo], axis=1), line, preferred_element_type=F32)
            row = lax.broadcasted_iota(jnp.int32, (8, PZ), 0)
            first, last = row == 0, row == 7
            for b in range(size):
                news = []
                for x in range(CX):
                    base = CY * x
                    t0, t1 = dcur[b, pl.ds(base, 8), :], dcur[b, pl.ds(base + 8, 8), :]
                    lo0 = jnp.where(first, t0, pltpu.roll(t0, 1, 0))
                    hi1 = jnp.where(last, t1, pltpu.roll(t1, 7, 0))
                    y0 = lo0 + dcur[b, pl.ds(base + 1, 8), :]
                    y1 = dcur[b, pl.ds(base + 7, 8), :] + hi1
                    xm, xp = max(x - 1, 0) * CY, min(x + 1, CX - 1) * CY
                    for h, yy in ((0, y0), (1, y1)):
                        q = pl.ds(base + 8 * h, 8)
                        xs = dcur[b, pl.ds(xm + 8 * h, 8), :] + dcur[b, pl.ds(xp + 8 * h, 8), :]
                        r = b * cells + base + 8 * h
                        total = xs + yy + zs_[r:r + 8]
                        news.append((q, acur[b, q, :] + bcur[b, q, :] * total))
                for q, v in news:
                    dcur[b, q, :] = v
            return 0

        lax.fori_loop(0, SWEEPS, sweep, 0)
        for b in range(size):
            res[first + b] = jnp.maximum(dcur[b].reshape(CX, CY, PZ), res[first + b])

    for m in range(FIRST):
        t_copy(m).wait_recv()
    arrived = first = 0
    for size, needed in STAGES:
        for m in range(arrived, needed):
            t_copy(FIRST + m).wait_recv()
        arrived = needed
        batch(first, size, arrived)
        first += size

    wait_sends(s_copy, (0, 1, 2, 3))
    wait_sends(lambda d, x: u_copy(u0, 0, d, x), (0, 1, 2, 3))
    wait_sends(lambda d, x: u_copy(u1, 1, d, x), (0, 1, 2, 3))
    wait_sends(lambda d, x: u_copy(u2, 2, d, x), (0, 2))
    for m in range(len(MOVES)):
        t_copy(m).wait_send()


def stencils(grid_mat, line_mat):
    shape = (CX * CY, CX * CY)
    r = lax.broadcasted_iota(jnp.int32, shape, 0)
    c = lax.broadcasted_iota(jnp.int32, shape, 1)
    rx, ry = r // CY, r % CY
    cx, cy = c // CY, c % CY
    one, zero = F32(1.0), F32(0.0)

    def at(x, y):
        return jnp.where(jnp.logical_and(cx == x, cy == y), one, zero)

    grid = at(jnp.minimum(rx + 1, CX - 1), ry) + at(jnp.maximum(rx - 1, 0), ry)
    grid = grid + at(rx, jnp.minimum(ry + 1, CY - 1)) + at(rx, jnp.maximum(ry - 1, 0))
    grid = grid.astype(jnp.bfloat16)
    grid_mat[...] = jnp.concatenate([grid, grid], axis=1)
    shape = (PZ, PZ)
    r = lax.broadcasted_iota(jnp.int32, shape, 0)
    c = lax.broadcasted_iota(jnp.int32, shape, 1)
    line = jnp.where(r == jnp.minimum(c + 1, PZ - 1), one, zero) + jnp.where(r == jnp.maximum(c - 1, 0), one, zero)
    line = line.astype(jnp.bfloat16)
    line_mat[...] = jnp.concatenate([line, line], axis=0)


def write_out(order, u2, hist, dmg, res, u_out, hist_out, dmg_out, out_sem):
    def zs(k):
        return pl.ds(pl.multiple_of(k * PZ, PZ), PZ)

    def copy(src, dst, n):
        return pltpu.make_async_copy(src, dst, out_sem.at[n])

    def start(k, _):
        copy(u2.at[:, pl.ds(1, CX), k + 1, pl.ds(R0, CY), :], u_out.at[:, :, :, zs(k)], 0).start()
        copy(hist.at[:, k], hist_out.at[:, :, zs(k)], 1).start()
        return 0

    lax.fori_loop(0, NZ, start, 0)

    def start_damage(k, _):
        def find(q, found):
            hit = order[0, q] == k
            return jnp.where(hit, q + 1, found)

        found = lax.fori_loop(0, PL, find, 0)

        @pl.when(found == 0)
        def _():
            copy(dmg.at[:, k], dmg_out.at[:, :, zs(k)], 2).start()

        @pl.when(found > 0)
        def _():
            copy(res.at[found - 1], dmg_out.at[:, :, zs(k)], 2).start()
        return 0

    lax.fori_loop(0, NZ, start_damage, 0)
    whole = u2.at[:, pl.ds(1, CX), pl.ds(1, NZ), pl.ds(R0, CY), :]
    copy(whole, whole, 0).wait()
    copy(hist, hist, 1).wait()
    copy(dmg, dmg, 2).wait()


ANY = pl.BlockSpec(memory_space=pl.ANY)


def body(displacement, force, damage, history_old, material, patch_ids, owners, toughness):
    size = (CX, CY, NZ * PZ)
    padded = (3, CX + 2, NZ + 2, R0 + CY + 8, PZ)
    inner = (CX, NZ, CY, PZ)
    tough = toughness[0]
    patch = (CX, CY, PZ)
    slots = (CAP,) + patch
    smem = pl.BlockSpec(memory_space=pltpu.SMEM)
    vmem = pl.BlockSpec(memory_space=pltpu.VMEM)
    dma = pltpu.SemaphoreType.DMA
    field, history, old, solved, order = pl.pallas_call(
        mechanics,
        out_shape=(
            pltpu.VMEM(padded, F32),
            pltpu.VMEM(inner, F32),
            pltpu.VMEM(inner, F32),
            pltpu.VMEM((PL,) + patch, F32),
            jax.ShapeDtypeStruct((1, PL), jnp.int32),
        ),
        in_specs=[smem] * 2 + [ANY] * 6,
        out_specs=(vmem,) * 4 + (smem,),
        scratch_shapes=[
            pltpu.VMEM(padded, F32), pltpu.VMEM(padded, F32),
            pltpu.VMEM(padded[1:], F32),
            pltpu.VMEM((3,) + inner, F32),
            pltpu.VMEM(inner, jnp.int32), pltpu.VMEM(inner, F32),
            pltpu.VMEM(inner, F32), pltpu.VMEM(inner, F32),
            pltpu.VMEM((N_YZ,) + slots, F32),
            pltpu.VMEM(slots, F32),
            [pltpu.VMEM(slots, F32)] * LATE,
            pltpu.VMEM((CX * CY, 2 * CX * CY), jnp.bfloat16),
            pltpu.VMEM((2 * PZ, PZ), jnp.bfloat16),
            pltpu.VMEM((BATCH, CX * CY, PZ), F32),
            pltpu.VMEM((BATCH, CX * CY, PZ), F32),
            pltpu.VMEM((BATCH, CX * CY, PZ), F32),
            pltpu.SMEM((4, PL), jnp.int32),
            dma((6,)),
            dma((4,)), dma((4,)),
            dma((3, 4)), dma((3, 4)),
            dma((len(MOVES),)), dma((len(MOVES),)),
        ],
        compiler_params=pltpu.CompilerParams(
            collective_id=0, has_side_effects=True, vmem_limit_bytes=50 << 20),
    )(patch_ids, owners[:, :, 0], displacement, force, damage, history_old, material, tough)

    return pl.pallas_call(
        write_out,
        out_shape=(
            jax.ShapeDtypeStruct((3,) + size, F32),
            jax.ShapeDtypeStruct(size, F32),
            jax.ShapeDtypeStruct(size, F32),
        ),
        in_specs=[smem] + [vmem] * 4,
        out_specs=(ANY, ANY, ANY),
        scratch_shapes=[dma((3,))],
        compiler_params=pltpu.CompilerParams(vmem_limit_bytes=8 << 20),
    )(order, field, history, old, solved)


def solution(mesh):
    return jax.shard_map(
        body,
        mesh=mesh,
        in_specs=(
            P(None, "gx", "yz", None),
            P(None, "gx", "yz", None),
            P("gx", "yz", None),
            P("gx", "yz", None),
            P("gx", "yz", None),
            P(("gx", "yz"), None),
            P(("gx", "yz"), None, None),
            P(("gx", "yz"), None, None, None, None, None),
        ),
        out_specs=(P(None, "gx", "yz", None), P("gx", "yz", None), P("gx", "yz", None)),
        check_vma=False,
    )
```

profile of v0, /device:TPU:58, one launch (start us, length us, event | category | flops | bytes accessed | tf_op | source)
XLA Modules:
  0.0 61.9 jit_solution(948261351944106542)
XLA Ops:
  0.6 57.7 %shard_map.103 = (f32[3,10,18,32,128]{4,3,2,1,0:T(8,128)S(1)}, f32[8,16,16,128]{3,2,1,0:T(8,128)S(1)}, f32[8,16,16,128]{3,2,1,0:T(8,128)S(1)}, f32[12,8,16,128]{3,2,1,0:T(8,128)S(1)}, s32[1,12]{1,0:T(1,128)}) custom-call(s32[1,12]{1,0:T(1,128)} %ids.1, s32[1,12]{1,0:T(1,128)} %bitcast.3, f32[3,8,16,2048]{3,2,1,0:T(8,128)} %disp.1, f32[3,8,16,2048]{3,2,1,0:T(8,128)} %force.1, ...), custom_call_target="tpu_custom_call" | custom-call | tf_op jit(solution)/shard_map/pallas_call | solution.py:522
  58.4 0.0 copy-start
  58.4 0.6 copy-done
  59.0 2.9 %shard_map.104 = (f32[3,8,16,2048]{3,2,1,0:T(8,128)}, f32[8,16,2048]{2,1,0:T(8,128)}, f32[8,16,2048]{2,1,0:T(8,128)}) custom-call(s32[1,12]{1,0:T(1,128)S(1)} %copy-done, f32[3,10,18,32,128]{4,3,2,1,0:T(8,128)S(1)} %get-tuple-element.9.u2, f32[8,16,16,128]{3,2,1,0:T(8,128)S(1)} %get-tuple-element.10.hist, f32[8,16,16,128]{3,2,1,0:T(8,128)S(1)} %get-tuple-element.11.dmg, ...), custom_call_target="tpu_custom_call" | custom-call | tf_op jit(solution)/shard_map/pallas_call | solution.py:557
Async XLA Ops:
  58.4 0.6 %copy-start = (s32[1,12]{1,0:T(1,128)S(1)}, s32[1,12]{1,0:T(1,128)}, u32[]{:S(2)}) copy-start(s32[1,12]{1,0:T(1,128)} %get-tuple-element.8.order) | copy-start | bytes 148
where the time goes:
time: 62 us; the launch traced here: 61.9 us
  Pallas kernels  60.6 us (98%)
  between operations  0.65 us (1%)
  local copies, waits for them, and re-layouts  0.62 us (1%)
    pallas_call x1, Pallas kernels, body(): pl.pallas_call(mechanics, out_shape=(pltpu.VMEM(padded, F32), pltpu.VMEM(...  57.7 us
    pallas_call x1, Pallas kernels, body(): pl.pallas_call(write_out, out_shape=(jax.ShapeDtypeStruct((3,) + size, F3...  2.86 us

commit v1 on v0

--- a/solution.py
+++ b/solution.py
@@ -45,8 +45,8 @@
     return lane == 0, lane == PZ - 1
 
 
-def mechanics(ids, own, disp, force, damage, hist_old, material, tough, u2, hist, dmg, res, order,
-              u0, u1, stiff, fbuf, mat, coef, wback, wahead, recv, home, late, grid_mat, line_mat, dcur, acur, bcur, keys,
+def mechanics(ids, own, disp, force, damage, hist_old, material, tough, u2, hist, fresh,
+              dmg, res, spot, u0, u1, stiff, fbuf, mat, coef, wback, wahead, recv, home, late, grid_mat, line_mat, dcur, acur, bcur, keys,
               ld_sem, s_send, s_recv, u_send, u_recv, t_send, t_recv):
     gx = lax.axis_index("gx")
     yz = lax.axis_index("yz")
@@ -366,11 +366,13 @@
 
     lax.fori_loop(0, PL, fill_order, 0)
 
-    def fill_ids(q, _):
-        order[0, q] = ids[0, keys[3, q]]
-        return 0
-
-    lax.fori_loop(0, PL, fill_ids, 0)
+    def fill_spot(k, _):
+        def find(q, found):
+            return jnp.where(ids[0, keys[3, q]] == k, q + 1, found)
+        spot[k] = lax.fori_loop(0, PL, find, 0)
+        return 0
+
+    lax.fori_loop(0, NZ, fill_spot, 0)
 
     mine.wait()
     cells = CX * CY
@@ -438,6 +440,13 @@
         batch(first, size, arrived)
         first += size
 
+    def settle(k, _):
+        place = spot[k]
+        fresh[k] = jnp.where(place > 0, res[jnp.maximum(place - 1, 0)], dmg[:, k])
+        return 0
+
+    lax.fori_loop(0, NZ, settle, 0)
+
     wait_sends(s_copy, (0, 1, 2, 3))
     wait_sends(lambda d, x: u_copy(u0, 0, d, x), (0, 1, 2, 3))
     wait_sends(lambda d, x: u_copy(u1, 1, d, x), (0, 1, 2, 3))
@@ -469,7 +478,7 @@
     line_mat[...] = jnp.concatenate([line, line], axis=0)
 
 
-def write_out(order, u2, hist, dmg, res, u_out, hist_out, dmg_out, out_sem):
+def write_out(u2, hist, fresh, u_out, hist_out, dmg_out, out_sem):
     def zs(k):
         return pl.ds(pl.multiple_of(k * PZ, PZ), PZ)
 
@@ -479,31 +488,14 @@
     def start(k, _):
         copy(u2.at[:, pl.ds(1, CX), k + 1, pl.ds(R0, CY), :], u_out.at[:, :, :, zs(k)], 0).start()
         copy(hist.at[:, k], hist_out.at[:, :, zs(k)], 1).start()
+        copy(fresh.at[k], dmg_out.at[:, :, zs(k)], 2).start()
         return 0
 
     lax.fori_loop(0, NZ, start, 0)
-
-    def start_damage(k, _):
-        def find(q, found):
-            hit = order[0, q] == k
-            return jnp.where(hit, q + 1, found)
-
-        found = lax.fori_loop(0, PL, find, 0)
-
-        @pl.when(found == 0)
-        def _():
-            copy(dmg.at[:, k], dmg_out.at[:, :, zs(k)], 2).start()
-
-        @pl.when(found > 0)
-        def _():
-            copy(res.at[found - 1], dmg_out.at[:, :, zs(k)], 2).start()
-        return 0
-
-    lax.fori_loop(0, NZ, start_damage, 0)
     whole = u2.at[:, pl.ds(1, CX), pl.ds(1, NZ), pl.ds(R0, CY), :]
     copy(whole, whole, 0).wait()
     copy(hist, hist, 1).wait()
-    copy(dmg, dmg, 2).wait()
+    copy(fresh, fresh, 2).wait()
 
 
 ANY = pl.BlockSpec(memory_space=pl.ANY)
@@ -519,18 +511,17 @@
     smem = pl.BlockSpec(memory_space=pltpu.SMEM)
     vmem = pl.BlockSpec(memory_space=pltpu.VMEM)
     dma = pltpu.SemaphoreType.DMA
-    field, history, old, solved, order = pl.pallas_call(
+    field, history, fresh = pl.pallas_call(
         mechanics,
         out_shape=(
             pltpu.VMEM(padded, F32),
             pltpu.VMEM(inner, F32),
-            pltpu.VMEM(inner, F32),
-            pltpu.VMEM((PL,) + patch, F32),
-            jax.ShapeDtypeStruct((1, PL), jnp.int32),
+            pltpu.VMEM((NZ,) + patch, F32),
         ),
         in_specs=[smem] * 2 + [ANY] * 6,
-        out_specs=(vmem,) * 4 + (smem,),
+        out_specs=(vmem,) * 3,
         scratch_shapes=[
+            pltpu.VMEM(inner, F32), pltpu.VMEM((PL,) + patch, F32), pltpu.SMEM((NZ,), jnp.int32),
             pltpu.VMEM(padded, F32), pltpu.VMEM(padded, F32),
             pltpu.VMEM(padded[1:], F32),
             pltpu.VMEM((3,) + inner, F32),
@@ -561,11 +552,11 @@
             jax.ShapeDtypeStruct(size, F32),
             jax.ShapeDtypeStruct(size, F32),
         ),
-        in_specs=[smem] + [vmem] * 4,
+        in_specs=[vmem] * 3,
         out_specs=(ANY, ANY, ANY),
         scratch_shapes=[dma((3,))],
         compiler_params=pltpu.CompilerParams(vmem_limit_bytes=8 << 20),
-    )(order, field, history, old, solved)
+    )(field, history, fresh)
 
 
 def solution(mesh):

time: 62 us -> 60.5 us (0.976)
  Pallas kernels: 60.6 us -> 59.7 us
  local copies, waits for them, and re-layouts: 0.62 us -> 0 us
where the time goes in v1:
time: 60.5 us; the launch traced here: 60.4 us
  Pallas kernels  59.7 us (99%)
  between operations  0.64 us (1%)
    pallas_call x1, Pallas kernels, body(): pl.pallas_call(mechanics, out_shape=(pltpu.VMEM(padded, F32), pltpu.VMEM(...  57.4 us
    pallas_call x1, Pallas kernels, body(): pl.pallas_call(write_out, out_shape=(jax.ShapeDtypeStruct((3,) + size, F3...  2.32 us

profile of v1, /device:TPU:58, one launch (start us, length us, event | category | flops | bytes accessed | tf_op | source)
XLA Modules:
  0.0 60.4 jit_solution(4224773430532367699)
XLA Ops:
  0.6 57.4 %shard_map.103 = (f32[3,10,18,32,128]{4,3,2,1,0:T(8,128)S(1)}, f32[8,16,16,128]{3,2,1,0:T(8,128)S(1)}, f32[16,8,16,128]{3,2,1,0:T(8,128)S(1)}) custom-call(s32[1,12]{1,0:T(1,128)} %ids.1, s32[1,12]{1,0:T(1,128)} %bitcast.3, f32[3,8,16,2048]{3,2,1,0:T(8,128)} %disp.1, f32[3,8,16,2048]{3,2,1,0:T(8,128)} %force.1, f32[8,16,2048]{2,1,0:T(8,128)} %damage.1, ...), custom_call_target="tpu_custom_call" | custom-call | tf_op jit(solution)/shard_map/pallas_call | solution.py:514
  58.1 2.3 %shard_map.104 = (f32[3,8,16,2048]{3,2,1,0:T(8,128)}, f32[8,16,2048]{2,1,0:T(8,128)}, f32[8,16,2048]{2,1,0:T(8,128)}) custom-call(f32[3,10,18,32,128]{4,3,2,1,0:T(8,128)S(1)} %get-tuple-element.6.u2, f32[8,16,16,128]{3,2,1,0:T(8,128)S(1)} %get-tuple-element.7.hist, f32[16,8,16,128]{3,2,1,0:T(8,128)S(1)} %get-tuple-element.8.fresh), custom_call_target="tpu_custom_call" | custom-call | tf_op jit(solution)/shard_map/pallas_call | solution.py:548
